TPU v7x, 512 devices: a whole 4x8x8 slice. The times are simulated.
512 devices in a mesh: leaf: 8 (over z), row: 8 (over y_lo, x), col: 8 (over y_hi, core).
Axes of the slice: x: 4, y: 8 (y_hi: 4, y_lo: 2; y = y_hi * 2 + y_lo), z: 8, core: 2. Of those that a mesh axis runs over, the one named last changes fastest.
Arguments:
- child_update: bfloat16 [8, 3072, 3072], P('leaf', 'row', 'col'), as said below
- block_map: int32 [8, 24], replicated, may hold values from 0 to 63, as said below
- pivot_entries: float32 [8, 4096, 512], P('leaf', 'row'), as said below
- pivot_count: int32 [4], replicated, may hold values from 256 to 512, as said below
Outputs:
- factor: float32 [8, 4096, 512], P('leaf', 'row')
- update: bfloat16 [8, 4096, 8192], P('leaf', 'row', 'col')
Inputs may be any that keep to these rules, and one draw needn't show every extreme that they name: `child_update`: each child's block is symmetric positive definite. `block_map`: each row lists 3072/128 distinct parent blocks in increasing order and includes the first and the last block; rows of odd children list, besides the first block, only blocks from 32 on. `pivot_entries`: the first 512 rows of each even leaf slice form a symmetric positive definite block. `pivot_count`: some parent has exactly 512 pivots.
All inputs are finite; a program needn't handle non-finite values.
Results may differ from a plain program's by a relative error of at most 0.01.
Values may be sent and summed in bfloat16 or wider, within the bound.
A program may use at most 64 MiB of HBM per device.

v0:
```python
import jax
import jax.numpy as jnp
from jax import lax
from jax.sharding import PartitionSpec as P

NF = 8192
BLK = 128
PMAX = 512


def from_partner(shard, axis, apart):
    return lax.ppermute(shard, axis, [(i, i ^ 1 << apart) for i in range(lax.axis_size(axis))])


def spread(value, axis, source):
    kept = jnp.where(lax.axis_index(axis) == source, value, 0).astype(value.dtype)
    return lax.psum(kept, axis)


def source_index(block_list, targets):
    matches = block_list[None, :] == (targets // BLK)[:, None]
    present = jnp.any(matches, axis=1)
    slots = jnp.arange(block_list.shape[0], dtype=jnp.int32)
    position = jnp.sum(jnp.where(matches, slots[None, :], 0), axis=1)
    return jnp.where(present, position * BLK + targets % BLK, -1)


def pick_entries(shard_piece, sources, along):
    extent = shard_piece.shape[along]
    inside = (sources >= 0) & (sources >= 0) & (sources < extent)
    picked = jnp.take(shard_piece, jnp.clip(sources, 0, extent - 1), axis=along).astype(jnp.float32)
    shaped = inside[:, None] if along == 0 else inside[None, :]
    return jnp.where(shaped, picked, 0.0)


def solve_rows(pivot_square, columns, pivot_mask):
    pivot_pair = pivot_mask[:, None] & pivot_mask[None, :]
    square = jnp.where(pivot_pair, pivot_square, jnp.eye(PMAX, dtype=jnp.float32))
    chol_lower = jnp.linalg.cholesky(square)
    return lax.linalg.triangular_solve(
        chol_lower, columns, left_side=False, lower=True, transpose_a=True
    )


def on_device(child_update, block_map, pivot_entries, pivot_count):
    leaf_id = lax.axis_index("leaf")
    half_id = leaf_id % 2
    parent_id = leaf_id // 2
    row_count = lax.axis_size("row")
    col_count = lax.axis_size("col")
    row_id = lax.axis_index("row")
    col_id = lax.axis_index("col")
    child_block = child_update[0]
    own_map = block_map[leaf_id]
    owner_rows = pivot_entries.shape[1]
    range_cols = NF // col_count
    half_rows = NF // 2
    steps_rows = jnp.arange(owner_rows, dtype=jnp.int32)
    row_targets = jnp.concatenate(
        [row_id * owner_rows + steps_rows, half_rows + row_id * owner_rows + steps_rows]
    )
    col_targets = col_id * range_cols + jnp.arange(range_cols, dtype=jnp.int32)
    row_sources = source_index(own_map, row_targets)
    col_sources = source_index(own_map, col_targets)
    strip = pick_entries(lax.all_gather(child_block, "col", axis=1, tiled=True), col_sources, 1)
    both_halves = pick_entries(
        lax.all_gather(strip.astype(jnp.bfloat16), "row", axis=0, tiled=True), row_sources, 0
    )
    both_halves = both_halves.astype(jnp.bfloat16)
    own_half = jnp.where(half_id == 0, both_halves[:owner_rows], both_halves[owner_rows:])
    other_half = jnp.where(half_id == 0, both_halves[owner_rows:], both_halves[:owner_rows])
    from_sibling = from_partner(other_half, "leaf", 0)
    assembled = own_half.astype(jnp.float32) + from_sibling.astype(jnp.float32)
    pivots = pivot_count[parent_id]
    pivot_mask = jnp.arange(PMAX, dtype=jnp.int32) < pivots
    local_columns = jnp.where(pivot_mask[None, :], assembled[:, :PMAX] + pivot_entries[0], 0.0)
    received = (
        from_partner(local_columns.astype(jnp.bfloat16), "leaf", 0).astype(local_columns.dtype),
        from_partner(local_columns.astype(jnp.bfloat16), "leaf", 0).astype(local_columns.dtype),
    )
    square_piece = jnp.where(half_id == 0, local_columns, received[0])
    lower_rows = jnp.where(half_id == 0, local_columns, received[1])
    upper_rows = jnp.where(half_id == 0, received[1], local_columns)
    pair_columns = jnp.concatenate([lower_rows, upper_rows], axis=0)
    pivot_square = spread(square_piece.astype(jnp.bfloat16), "row", 0).astype(square_piece.dtype)
    factor_pair = spread(solve_rows(pivot_square, pair_columns, pivot_mask), "col", 0)
    factor_rows = jnp.where(half_id == 0, factor_pair[:owner_rows], factor_pair[owner_rows:])
    rounded_pair = factor_pair.astype(jnp.bfloat16)
    rounded = jnp.where(half_id == 0, rounded_pair[:owner_rows], rounded_pair[owner_rows:])
    per_range = range_cols // owner_rows
    first_owner = col_id * per_range
    owner_half = first_owner // row_count
    range_source = jnp.where(owner_half == 0, rounded_pair[:owner_rows], rounded_pair[owner_rows:])
    gathered = []
    for part_id in range(per_range):
        gathered.append(spread(range_source, "row", (first_owner + part_id) % row_count))
    far_rows = jnp.concatenate(gathered, axis=0)
    product = lax.dot_general(
        rounded, far_rows, (((1,), (1,)), ((), ())), preferred_element_type=jnp.float32
    )
    schur_part = assembled - product
    row_true = half_id * half_rows + row_id * owner_rows + steps_rows
    keep_rows = row_true >= pivots
    keep_cols = col_targets >= pivots
    update = jnp.where(keep_rows[:, None] & keep_cols[None, :], schur_part, 0.0).astype(
        jnp.bfloat16
    )
    return (factor_rows[None], update[None])


def solution(mesh):
    return jax.shard_map(
        on_device,
        mesh=mesh,
        in_specs=(P("leaf", "row", "col"), P(), P("leaf", "row", None), P()),
        out_specs=(P("leaf", "row", None), P("leaf", "row", "col")),
        check_vma=False,
    )
```

profile of v0, /device:TPU:16, one launch (start us, length us, event | category | flops | bytes accessed | tf_op | source)
XLA Modules:
  0.0 648.8 jit_solution(12378663692728715487)
XLA Ops:
  9.6 45.9 %all-gather.6.cloned.1.call-done = bf16[1,384,3072]{1,2,0:T(8,128)(2,1)} async-done(((bf16[1,384,384]{1,2,0:T(8,128)(2,1)}), bf16[1,384,3072]{1,2,0:T(8,128)(2,1)}) %all-gather.6.cloned.1.call-update) | async-done | bytes 2359312 | tf_op jit(solution)/shard_map/all_gather | solution.py:65
  55.5 5.7 gather_fusion
  62.6 75.8 %all-gather.4.cloned.1.call-done = bf16[3072,1024]{0,1:T(8,128)(2,1)} async-done(((bf16[384,1024]{0,1:T(8,128)(2,1)}), bf16[3072,1024]{0,1:T(8,128)(2,1)}) %all-gather.4.cloned.1.call-update) | async-done | bytes 6291472 | tf_op jit(solution)/shard_map/all_gather | solution.py:67
  138.4 8.6 %copy.39 = bf16[3072,1024]{1,0:T(8,128)(2,1)} copy(bf16[3072,1024]{0,1:T(8,128)(2,1)} %all-gather.4.cloned.1.call-done) | data formatting | bytes 12582912 | tf_op jit(solution)/shard_map/all_gather | solution.py:67
  147.1 8.6 %gather_fusion.1 = bf16[1024,1024]{1,0:T(8,128)(2,1)S(1)} fusion(bf16[3072,1024]{1,0:T(8,128)(2,1)} %copy.39, s32[1024]{0:T(1024)S(1)} %broadcast_clamp_fusion), kind=kCustom, calls=%fused_computation.1 | custom fusion | bytes 4198400 | tf_op jit(solution)/shard_map/jit(_take)/gather | solution.py:31
  155.6 2.6 copy.40
  158.2 2.2 select_convert_fusion
  161.5 3.5 collective-permute-start
  167.6 20.9 %collective-permute-done = bf16[512,1024]{0,1:T(8,128)(2,1)} collective-permute-done((bf16[512,1024]{0,1:T(8,128)(2,1)}, bf16[512,1024]{0,1:T(8,128)(2,1)}, u32[]{:S(2)}, u32[]{:S(2)}) %collective-permute-start) | collective-permute-done | bytes 1048608 | tf_op jit(solution)/shard_map/ppermute | solution.py:12
  191.7 3.6 collective-permute-start.1
  195.3 11.0 %collective-permute-done.1 = bf16[512,512]{0,1:T(8,128)(2,1)S(1)} collective-permute-done((bf16[512,512]{0,1:T(8,128)(2,1)S(1)}, bf16[512,512]{0,1:T(8,128)(2,1)S(1)}, u32[]{:S(2)}, u32[]{:S(2)}) %collective-permute-start.1) | collective-permute-done | bytes 524320 | tf_op jit(solution)/shard_map/ppermute | solution.py:12
  209.1 83.1 %all-reduce.6.cloned.1.call-done = bf16[512,512]{0,1:T(8,128)(2,1)} async-done(((bf16[512,512]{0,1:T(8,128)(2,1)}), bf16[512,512]{0,1:T(8,128)(2,1)}) %all-reduce.6.cloned.1.call-update) | async-done | bytes 524304 | tf_op jit(solution)/shard_map/psum | solution.py:17
  292.2 2.2 convert_select_fusion.2
  298.3 11.7 %cholesky.103 = f32[128,128]{1,0:T(8,128)S(1)} custom-call(f32[128,128]{1,0:T(8,128)S(1)} %cholesky.263), custom_call_target="Cholesky" | custom-call | tf_op jit(solution)/shard_map/jit(cholesky)/cholesky | solution.py:39
  310.0 9.8 %custom-call.30 = f32[1,128,128]{1,2,0:T(8,128)S(1)} custom-call(f32[1,128,128]{2,1,0:T(8,128)S(1)} %get-tuple-element.59), custom_call_target="InvertDiagBlocksLowerTriangular" | custom-call | tf_op jit(solution)/shard_map/jit(cholesky)/cholesky | solution.py:39
  322.4 11.7 %cholesky.215 = f32[128,128]{1,0:T(8,128)S(1)} custom-call(f32[128,128]{1,0:T(8,128)S(1)} %cholesky.267), custom_call_target="Cholesky" | custom-call | tf_op jit(solution)/shard_map/jit(cholesky)/cholesky | solution.py:39
  335.7 10.6 %custom-call.31 = f32[1,128,128]{1,2,0:T(8,128)} custom-call(f32[1,128,128]{2,1,0:T(8,128)S(1)} %get-tuple-element.57), custom_call_target="InvertDiagBlocksLowerTriangular" | custom-call | tf_op jit(solution)/shard_map/jit(cholesky)/cholesky | solution.py:39
  350.8 11.7 %cholesky.236 = f32[128,128]{1,0:T(8,128)S(1)} custom-call(f32[128,128]{1,0:T(8,128)S(1)} %cholesky.272), custom_call_target="Cholesky" | custom-call | tf_op jit(solution)/shard_map/jit(cholesky)/cholesky | solution.py:39
  362.6 9.8 %custom-call.32 = f32[1,128,128]{1,2,0:T(8,128)S(1)} custom-call(f32[1,128,128]{2,1,0:T(8,128)S(1)} %get-tuple-element.55), custom_call_target="InvertDiagBlocksLowerTriangular" | custom-call | tf_op jit(solution)/shard_map/jit(cholesky)/cholesky | solution.py:39
  374.1 11.9 %cholesky.253 = f32[128,128]{1,0:T(8,128)S(1)} custom-call(f32[128,128]{1,0:T(8,128)S(1)} %convolution_subtract_fusion.2), custom_call_target="Cholesky" | custom-call | tf_op jit(solution)/shard_map/jit(cholesky)/cholesky | solution.py:39
  392.3 14.3 %while.1 = (s32[]{:T(128)}, f32[512,512]{0,1:T(8,128)}, s32[4,2]{0,1:T(2,128)S(1)}, f32[4,128,128]{2,1,0:T(8,128)}, s32[]{:T(128)}) while((s32[]{:T(128)}, f32[512,512]{0,1:T(8,128)}, s32[4,2]{0,1:T(2,128)S(1)}, f32[4,128,128]{2,1,0:T(8,128)}, s32[]{:T(128)}) %tuple.40), condition=%wide.while_cond, body=%wide.while_body.sunk | while | flops 2 | bytes 393829 | solution.py:40
  392.9 2.3 dynamic-slice.7
  396.5 2.3 dynamic-slice.7
  400.1 2.3 dynamic-slice.7
  403.7 2.2 dynamic-slice.7
  406.6 40.1 %custom-call.33 = f32[4,128,128]{1,2,0:T(8,128)S(1)} custom-call(f32[4,128,128]{2,1,0:T(8,128)} %get-tuple-element.9), custom_call_target="InvertDiagBlocksLowerTriangular" | custom-call | tf_op jit(solution)/shard_map/triangular_solve | solution.py:40
  451.8 2.1 fusion
  456.2 88.2 %all-reduce.8.cloned.1.call-done = f32[1024,512]{0,1:T(8,128)} async-done(((f32[1024,512]{0,1:T(8,128)}), f32[1024,512]{0,1:T(8,128)}) %all-reduce.8.cloned.1.call-update) | async-done | bytes 2097168 | tf_op jit(solution)/shard_map/psum | solution.py:17
  549.7 2.7 copy.55
  552.3 84.4 %all-reduce.10.cloned.1.call-done = (bf16[512,512]{0,1:T(8,128)(2,1)}, bf16[512,512]{0,1:T(8,128)(2,1)}) async-done(((bf16[512,512]{0,1:T(8,128)(2,1)}, bf16[512,512]{0,1:T(8,128)(2,1)}), (bf16[512,512]{0,1:T(8,128)(2,1)}, bf16[512,512]{0,1:T(8,128)(2,1)})) %all-reduce.10.cloned.1.call-update) | async-done | bytes 1048592 | tf_op jit(solution)/shard_map/psum | solution.py:17
  636.7 3.0 fusion.6
  639.7 2.3 copy.56
  (115 shorter events, 49.0 us)
Async XLA Ops:
  7.2 2.0 copy-start
  7.2 48.3 %all-gather.6.cloned.1.call-start = ((), (), s32[]{:S(2)}) async-start(), calls=%async_computation.3 | async-start | bytes 2654208 | tf_op jit(solution)/shard_map/all_gather | solution.py:65
  9.1 129.3 %all-gather.4.cloned.1.call-start = ((), (), s32[]{:S(2)}) async-start(), calls=%async_computation | async-start | bytes 7077888 | tf_op jit(solution)/shard_map/all_gather | solution.py:67
  62.4 229.7 %all-reduce.6.cloned.1.call-start = ((), (), s32[]{:S(2)}) async-start(), calls=%async_computation.1 | async-start | bytes 1048576 | tf_op jit(solution)/shard_map/psum | solution.py:17
  160.4 4.7 copy-start.7
  160.4 6.0 copy-start.8
  161.5 26.9 %collective-permute-start = (bf16[512,1024]{0,1:T(8,128)(2,1)}, bf16[512,1024]{0,1:T(8,128)(2,1)}, u32[]{:S(2)}, u32[]{:S(2)}) collective-permute-start(bf16[512,1024]{0,1:T(8,128)(2,1)} %broadcast_select_fusion), channel_id=1, source_target_pairs={{0,64},{64,0},{128,192},{192,128},{256,320},{320,256},{384,448},{4... | collective-permute-start | bytes 3145736 | tf_op jit(solution)/shard_map/ppermute | solution.py:12
  167.6 23.9 %copy-start.4 = (f32[1,512,512]{1,2,0:T(8,128)S(1)}, f32[1,512,512]{1,2,0:T(8,128)}, u32[]{:S(2)}) copy-start(f32[1,512,512]{1,2,0:T(8,128)} %copy.41) | copy-start | bytes 3145732
  190.1 1.4 copy-start.2
  191.7 14.5 %collective-permute-start.1 = (bf16[512,512]{0,1:T(8,128)(2,1)S(1)}, bf16[512,512]{0,1:T(8,128)(2,1)S(1)}, u32[]{:S(2)}, u32[]{:S(2)}) collective-permute-start(bf16[512,512]{0,1:T(8,128)(2,1)S(1)} %get-tuple-element.44), channel_id=1, source_target_pairs={{0,64},{64,0},{128,192},{192,128},{256,320},{320,256},{384,448},{4... | collective-permute-start | bytes 1572872 | tf_op jit(solution)/shard_map/ppermute | solution.py:12
  206.3 1.6 copy-start.6
  207.3 337.1 %all-reduce.8.cloned.1.call-start = ((), (), s32[]{:S(2)}) async-start(), calls=%async_computation.2 | async-start | bytes 4194304 | tf_op jit(solution)/shard_map/psum | solution.py:17
  297.3 1.0 copy-start.5
  456.1 180.6 %all-reduce.10.cloned.1.call-start = ((), (), s32[]{:S(2)}) async-start(), calls=%async_computation.4 | async-start | bytes 2097152 | tf_op jit(solution)/shard_map/psum | solution.py:17
  546.2 2.3 copy-start.1
  549.6 87.1 %copy-start.3 = (f32[512,1024]{0,1:T(8,128)S(1)}, f32[512,1024]{0,1:T(8,128)}, u32[]{:S(2)}) copy-start(f32[512,1024]{0,1:T(8,128)} %copy-done.2) | copy-start | bytes 6291460
Sparse Core Ops, SparseCore 0:
  10.7 44.7 all-gather.5
  62.6 75.8 all-gather.3
  207.4 84.7 all-reduce.5
  456.2 88.1 all-reduce.7
  547.4 89.2 all-reduce.9
where the time goes:
time: 655 us; the launch traced here: 649 us
  waiting for transfers between devices  409 us (62%)
  other arithmetic  141 us (22%)
  local copies, waits for them, and re-layouts  56 us (9%)
  matrix products  17.5 us (3%)
  between operations  17.1 us (3%)
  starting transfers between devices  7.77 us (1%)
    psum x3, waiting for transfers between devices, spread(): return lax.psum(kept, axis)  256 us
    another operation x15, other arithmetic, solve_rows(): chol_lower = jnp.linalg.cholesky(square)  79.9 us
    all_gather x1, waiting for transfers between devices, on_device(): lax.all_gather(strip.astype(jnp.bfloat16), 'row', axis=0, tiled=True)  75.8 us
    all_gather x1, waiting for transfers between devices, on_device(): lax.all_gather(child_block, 'col', axis=1, tiled=True)  45.9 us
    another operation x3, other arithmetic, solve_rows(): lax.linalg.triangular_solve(chol_lower, columns, left_side=False, lower=T...  41.2 us
    ppermute x2, waiting for transfers between devices, from_partner(): lax.ppermute(shard, axis, [(i, i ^ 1 << apart) for i in range(lax.axis_si...  31.8 us
    gather x3, local copies, waits for them, and re-layouts, pick_entries(): jnp.take(shard_piece, jnp.clip(sources, 0, extent - 1), axis=along)  16.9 us
    another operation x20, local copies, waits for them, and re-layouts  14.2 us
  transfers between devices with their start and end apart: 7, of which 7 were waited for; matrix products, arithmetic and copies ran while one was open for 1% of the time, Pallas kernels for 0%

commit v1 on v0

--- a/solution.py
+++ b/solution.py
@@ -14,7 +14,7 @@
 
 def spread(value, axis, source):
     kept = jnp.where(lax.axis_index(axis) == source, value, 0).astype(value.dtype)
-    return lax.psum(kept, axis)
+    return jnp.sum(lax.all_gather(kept, axis), axis=0)
 
 
 def source_index(block_list, targets):

time: 655 us -> 749 us (1.14)
  the two profiles are of different devices: /device:TPU:16 before, /device:TPU:1 now
where the time goes in v1:
time: 749 us; the launch traced here: 741 us
  waiting for transfers between devices  472 us (63%)
  other arithmetic  156 us (21%)
  local copies, waits for them, and re-layouts  73.3 us (10%)
  between operations  17.6 us (2%)
  matrix products  15.3 us (2%)
    all_gather x4, waiting for transfers between devices, spread(): return jnp.sum(lax.all_gather(kept, axis), axis=0)  318 us
    another operation x15, other arithmetic, solve_rows(): chol_lower = jnp.linalg.cholesky(square)  80.1 us
    all_gather x1, waiting for transfers between devices, on_device(): lax.all_gather(strip.astype(jnp.bfloat16), 'row', axis=0, tiled=True)  75 us
    all_gather x1, waiting for transfers between devices, on_device(): lax.all_gather(child_block, 'col', axis=1, tiled=True)  47.6 us
    another operation x3, other arithmetic, solve_rows(): lax.linalg.triangular_solve(chol_lower, columns, left_side=False, lower=T...  41.2 us
    ppermute x2, waiting for transfers between devices, from_partner(): lax.ppermute(shard, axis, [(i, i ^ 1 << apart) for i in range(lax.axis_si...  30.6 us
    unnamed x25, local copies, waits for them, and re-layouts  22.6 us
    reduce_sum x4, other arithmetic, spread(): return jnp.sum(lax.all_gather(kept, axis), axis=0)  18.9 us
  transfers between devices with their start and end apart: 8, of which 8 were waited for; matrix products, arithmetic and copies ran while one was open for 2% of the time, Pallas kernels for 0%

profile of v1, /device:TPU:1, one launch (start us, length us, event | category | flops | bytes accessed | tf_op | source)
XLA Modules:
  0.0 741.0 jit_solution(13909162795094355962)
XLA Ops:
  9.6 47.6 %all-gather.15.cloned.1.call-done = bf16[1,384,3072]{1,2,0:T(8,128)(2,1)} async-done(((bf16[1,384,384]{1,2,0:T(8,128)(2,1)}), bf16[1,384,3072]{1,2,0:T(8,128)(2,1)}) %all-gather.15.cloned.1.call-update) | async-done | bytes 2359312 | tf_op jit(solution)/shard_map/all_gather | solution.py:65
  57.1 5.7 gather_fusion
  64.3 75.0 %all-gather.11.cloned.1.call-done = bf16[3072,1024]{0,1:T(8,128)(2,1)} async-done(((bf16[384,1024]{0,1:T(8,128)(2,1)}), bf16[3072,1024]{0,1:T(8,128)(2,1)}) %all-gather.11.cloned.1.call-update) | async-done | bytes 6291472 | tf_op jit(solution)/shard_map/all_gather | solution.py:67
  139.3 8.6 %copy.86 = bf16[3072,1024]{1,0:T(8,128)(2,1)} copy(bf16[3072,1024]{0,1:T(8,128)(2,1)} %all-gather.11.cloned.1.call-done) | data formatting | bytes 12582912 | tf_op jit(solution)/shard_map/all_gather | solution.py:67
  147.9 8.6 %gather_fusion.1 = bf16[1024,1024]{1,0:T(8,128)(2,1)S(1)} fusion(bf16[3072,1024]{1,0:T(8,128)(2,1)} %copy.86, s32[1024]{0:T(1024)S(1)} %broadcast_clamp_fusion), kind=kCustom, calls=%fused_computation.1 | custom fusion | bytes 4198400 | tf_op jit(solution)/shard_map/jit(_take)/gather | solution.py:31
  156.5 2.6 copy.87
  162.3 3.3 collective-permute-start
  168.2 20.2 %collective-permute-done = bf16[512,1024]{0,1:T(8,128)(2,1)} collective-permute-done((bf16[512,1024]{0,1:T(8,128)(2,1)}, bf16[512,1024]{0,1:T(8,128)(2,1)}, u32[]{:S(2)}, u32[]{:S(2)}) %collective-permute-start) | collective-permute-done | bytes 1048608 | tf_op jit(solution)/shard_map/ppermute | solution.py:12
  191.7 3.3 collective-permute-start.1
  195.0 10.4 %collective-permute-done.1 = bf16[512,512]{0,1:T(8,128)(2,1)S(1)} collective-permute-done((bf16[512,512]{0,1:T(8,128)(2,1)S(1)}, bf16[512,512]{0,1:T(8,128)(2,1)S(1)}, u32[]{:S(2)}, u32[]{:S(2)}) %collective-permute-start.1) | collective-permute-done | bytes 524320 | tf_op jit(solution)/shard_map/ppermute | solution.py:12
  208.3 56.6 %all-gather.17.cloned.1.call-done = bf16[4096,512]{0,1:T(8,128)(2,1)} async-done(((bf16[512,512]{0,1:T(8,128)(2,1)}), bf16[4096,512]{0,1:T(8,128)(2,1)}) %all-gather.17.cloned.1.call-update) | async-done | bytes 4194320 | tf_op jit(solution)/shard_map/all_gather | solution.py:17
  265.0 4.4 copy.116
  269.4 3.3 bitcast_reduce_fusion.2
  273.9 2.5 copy.90
  278.9 11.7 %cholesky.103 = f32[128,128]{1,0:T(8,128)S(1)} custom-call(f32[128,128]{1,0:T(8,128)S(1)} %cholesky.263), custom_call_target="Cholesky" | custom-call | tf_op jit(solution)/shard_map/jit(cholesky)/cholesky | solution.py:39
  290.6 9.8 %custom-call.30 = f32[1,128,128]{1,2,0:T(8,128)S(1)} custom-call(f32[1,128,128]{2,1,0:T(8,128)S(1)} %get-tuple-element.69), custom_call_target="InvertDiagBlocksLowerTriangular" | custom-call | tf_op jit(solution)/shard_map/jit(cholesky)/cholesky | solution.py:39
  303.0 12.1 %cholesky.215 = f32[128,128]{1,0:T(8,128)S(1)} custom-call(f32[128,128]{1,0:T(8,128)S(1)} %cholesky.267), custom_call_target="Cholesky" | custom-call | tf_op jit(solution)/shard_map/jit(cholesky)/cholesky | solution.py:39
  316.7 10.4 %custom-call.31 = f32[1,128,128]{1,2,0:T(8,128)} custom-call(f32[1,128,128]{2,1,0:T(8,128)S(1)} %get-tuple-element.67), custom_call_target="InvertDiagBlocksLowerTriangular" | custom-call | tf_op jit(solution)/shard_map/jit(cholesky)/cholesky | solution.py:39
  331.6 11.7 %cholesky.236 = f32[128,128]{1,0:T(8,128)S(1)} custom-call(f32[128,128]{1,0:T(8,128)S(1)} %cholesky.272), custom_call_target="Cholesky" | custom-call | tf_op jit(solution)/shard_map/jit(cholesky)/cholesky | solution.py:39
  343.5 9.8 %custom-call.32 = f32[1,128,128]{1,2,0:T(8,128)S(1)} custom-call(f32[1,128,128]{2,1,0:T(8,128)S(1)} %get-tuple-element.65), custom_call_target="InvertDiagBlocksLowerTriangular" | custom-call | tf_op jit(solution)/shard_map/jit(cholesky)/cholesky | solution.py:39
  355.0 11.8 %cholesky.253 = f32[128,128]{1,0:T(8,128)S(1)} custom-call(f32[128,128]{1,0:T(8,128)S(1)} %convolution_subtract_fusion.2), custom_call_target="Cholesky" | custom-call | tf_op jit(solution)/shard_map/jit(cholesky)/cholesky | solution.py:39
  373.0 14.3 %while.1 = (s32[]{:T(128)}, f32[512,512]{0,1:T(8,128)}, s32[4,2]{0,1:T(2,128)S(1)}, f32[4,128,128]{2,1,0:T(8,128)}, s32[]{:T(128)}) while((s32[]{:T(128)}, f32[512,512]{0,1:T(8,128)}, s32[4,2]{0,1:T(2,128)S(1)}, f32[4,128,128]{2,1,0:T(8,128)}, s32[]{:T(128)}) %tuple.45), condition=%wide.while_cond, body=%wide.while_body.sunk | while | flops 2 | bytes 393829 | solution.py:40
  387.3 40.1 %custom-call.33 = f32[4,128,128]{1,2,0:T(8,128)S(1)} custom-call(f32[4,128,128]{2,1,0:T(8,128)} %get-tuple-element.9), custom_call_target="InvertDiagBlocksLowerTriangular" | custom-call | tf_op jit(solution)/shard_map/triangular_solve | solution.py:40
  437.5 159.2 %all-gather.13.cloned.1.call-done = f32[8,1024,512]{2,1,0:T(8,128)} async-done(((f32[1,1024,512]{2,1,0:T(8,128)}), f32[8,1024,512]{2,1,0:T(8,128)}) %all-gather.13.cloned.1.call-update) | async-done | bytes 16777232 | tf_op jit(solution)/shard_map/all_gather | solution.py:17
  596.8 9.4 %reduce_sum.66 = f32[1024,512]{1,0:T(8,128)} reduce(f32[8,1024,512]{2,1,0:T(8,128)} %all-gather.13.cloned.1.call-done, f32[]{:T(128)} %constant.284.clone.1), dimensions={0}, to_apply=%region_13.14 | reduce | flops 3670016 | bytes 18874372 | tf_op jit(solution)/shard_map/reduce_sum | solution.py:17
  611.8 2.5 copy.107
  614.3 51.1 %all-gather.21.cloned.1.call-done = bf16[4096,512]{0,1:T(8,128)(2,1)} async-done(((bf16[512,512]{0,1:T(8,128)(2,1)}), bf16[4096,512]{0,1:T(8,128)(2,1)}) %all-gather.21.cloned.1.call-update) | async-done | bytes 4194320 | tf_op jit(solution)/shard_map/all_gather | solution.py:17
  665.4 4.4 copy.118
  669.8 3.1 bitcast_reduce_fusion
  672.9 51.1 %all-gather.19.cloned.1.call-done = bf16[4096,512]{0,1:T(8,128)(2,1)} async-done(((bf16[512,512]{0,1:T(8,128)(2,1)}), bf16[4096,512]{0,1:T(8,128)(2,1)}) %all-gather.19.cloned.1.call-update) | async-done | bytes 4194320 | tf_op jit(solution)/shard_map/all_gather | solution.py:17
  724.1 4.4 copy.117
  728.5 3.1 bitcast_reduce_fusion.1
  (128 shorter events, 65.3 us)
Async XLA Ops:
  7.2 2.0 copy-start
  7.2 50.0 %all-gather.15.cloned.1.call-start = ((), (), s32[]{:S(2)}) async-start(), calls=%async_computation.2 | async-start | bytes 2654208 | tf_op jit(solution)/shard_map/all_gather | solution.py:65
  9.1 130.2 %all-gather.11.cloned.1.call-start = ((), (), s32[]{:S(2)}) async-start(), calls=%async_computation | async-start | bytes 7077888 | tf_op jit(solution)/shard_map/all_gather | solution.py:67
  64.1 200.8 %all-gather.17.cloned.1.call-start = ((), (), s32[]{:S(2)}) async-start(), calls=%async_computation.3 | async-start | bytes 4718592 | tf_op jit(solution)/shard_map/all_gather | solution.py:17
  161.2 4.4 copy-start.7
  161.2 5.7 copy-start.8
  162.3 26.1 %collective-permute-start = (bf16[512,1024]{0,1:T(8,128)(2,1)}, bf16[512,1024]{0,1:T(8,128)(2,1)}, u32[]{:S(2)}, u32[]{:S(2)}) collective-permute-start(bf16[512,1024]{0,1:T(8,128)(2,1)} %broadcast_select_fusion), channel_id=1, source_target_pairs={{0,64},{64,0},{128,192},{192,128},{256,320},{320,256},{384,448},{4... | collective-permute-start | bytes 3145736 | tf_op jit(solution)/shard_map/ppermute | solution.py:12
  168.2 23.3 %copy-start.4 = (f32[1,512,512]{1,2,0:T(8,128)S(1)}, f32[1,512,512]{1,2,0:T(8,128)}, u32[]{:S(2)}) copy-start(f32[1,512,512]{1,2,0:T(8,128)} %copy.88) | copy-start | bytes 3145732
  190.1 1.4 copy-start.2
  191.7 13.7 %collective-permute-start.1 = (bf16[512,512]{0,1:T(8,128)(2,1)S(1)}, bf16[512,512]{0,1:T(8,128)(2,1)S(1)}, u32[]{:S(2)}, u32[]{:S(2)}) collective-permute-start(bf16[512,512]{0,1:T(8,128)(2,1)S(1)} %get-tuple-element.54), channel_id=1, source_target_pairs={{0,64},{64,0},{128,192},{192,128},{256,320},{320,256},{384,448},{4... | collective-permute-start | bytes 1572872 | tf_op jit(solution)/shard_map/ppermute | solution.py:12
  205.4 1.7 copy-start.6
  206.4 390.4 %all-gather.13.cloned.1.call-start = ((), (), s32[]{:S(2)}) async-start(), calls=%async_computation.1 | async-start | bytes 18874368 | tf_op jit(solution)/shard_map/all_gather | solution.py:17
  277.9 1.0 copy-start.5
  437.2 228.2 %all-gather.21.cloned.1.call-start = ((), (), s32[]{:S(2)}) async-start(), calls=%async_computation.5 | async-start | bytes 4718592 | tf_op jit(solution)/shard_map/all_gather | solution.py:17
  609.4 114.7 %all-gather.19.cloned.1.call-start = ((), (), s32[]{:S(2)}) async-start(), calls=%async_computation.4 | async-start | bytes 4718592 | tf_op jit(solution)/shard_map/all_gather | solution.py:17
  728.5 3.1 copy-start.3
  731.6 2.2 copy-start.1
Sparse Core Ops, SparseCore 0:
  10.7 46.4 all-gather.14
  64.3 74.9 all-gather.10
  206.5 58.3 all-gather.16
  437.4 159.3 all-gather.12
  609.5 55.8 all-gather.20
  667.4 56.6 all-gather.18
